TPU v7x, 128 devices: a whole 4x4x4 slice. The times are simulated.
128 devices in a mesh: unit: 16 (over x, y), tm: 8 (over z, core).
Axes of the slice: x: 4, y: 4, z: 4, core: 2. Of those that a mesh axis runs over, the one named last changes fastest.
Arguments:
- spikes: int32 [4096, 16384], P('tm', 'unit'), may hold values from 0 to 2
- stimulus: bfloat16 [4096, 64], P('tm'), may hold values from -6 to 6
- bias: float32 [16384], P('unit'), may hold values from -1.5 to 0
- hist_weight: float32 [10, 16384], P(None, 'unit'), may hold values from -0.9 to 0.9
- stim_filter: bfloat16 [16384, 64], P('unit'), may hold values from -0.5 to 0.5
- coupling_mix: float32 [10], replicated, may hold values from -3 to 3
- coupling_target: int32 [128, 4], P('unit'), may hold values from 0 to 127, as said below
- coupling_weight: bfloat16 [128, 4, 128, 128], P('unit'), may hold values from -0.059814453 to 0.059814453
Outputs:
- grad_bias: float32 [16384], P('unit')
- grad_hist: float32 [10, 16384], P(None, 'unit')
- grad_stim: float32 [16384, 64], P(('unit', 'tm'))
- grad_coupling: float32 [128, 4, 128, 128], P('unit', None, 'tm')
Inputs may be any that keep to these rules, and one draw needn't show every extreme that they name: `coupling_target`: the 4 entries of a row are distinct. Among the rows of one device (8 aligned rows), the targets owned by any one device (tiles k * 8 to k * 8 + 7) are at most 2 distinct tiles, and every owner that is named gets exactly 2.
All inputs are finite; a program needn't handle non-finite values.
Results may differ from a plain program's by a relative error of at most 0.0041.
Values may be sent and summed in bfloat16 or wider, within the bound.
A program may use at most 256 MiB of HBM per device.

v0:
```python
import math
import jax
import jax.numpy as jnp
from jax import lax
from jax.sharding import PartitionSpec as P

TILE = 128
FAN = 4
CAP = 2
NB = 10
LAG = 128


def passed_along(value, axis, steps):
    count = lax.axis_size(axis)
    leading, last = (max(0, -steps), min(count, count - steps))
    return lax.ppermute(value, axis, [(source, source + steps) for source in range(leading, last)])


def raised_cosine(count, lag):
    low = math.log(2.0)
    high = math.log(lag + 1.0)
    spacing = (high - low) / (count - 1)
    stretched = jnp.log(jnp.arange(1, lag + 1).astype(jnp.float32) + 1.0)
    centers = low + spacing * jnp.arange(count).astype(jnp.float32)
    phases = jnp.clip(
        (stretched[None, :] - centers[:, None]) * (math.pi / (2.0 * spacing)), -math.pi, math.pi
    )
    shapes = 0.5 * (1.0 + jnp.cos(phases))
    return (shapes / jnp.sum(shapes, axis=1, keepdims=True)).astype(jnp.bfloat16)


def shards(
    spikes, stimulus, bias, hist_weight, stim_filter, coupling_mix, coupling_target, coupling_weight
):
    time_dev, units_dev = spikes.shape
    tiles_dev = units_dev // TILE
    unit_count = lax.axis_size("unit")
    time_count = lax.axis_size("tm")
    time_total = time_dev * time_count
    block_rows = min(time_dev, 4 * LAG)
    counts_bf = spikes.astype(jnp.bfloat16)
    previous = passed_along(counts_bf[time_dev - LAG :], "tm", 1)
    extended = jnp.concatenate([previous, counts_bf], axis=0)
    basis = raised_cosine(NB, LAG)
    row_index = jnp.arange(block_rows, dtype=jnp.int32)[:, None]
    col_index = jnp.arange(block_rows + LAG, dtype=jnp.int32)[None, :]
    lag_index = LAG + row_index - col_index
    inside = (lag_index >= 1) & (lag_index <= LAG)
    toeplitz = jnp.where(
        inside[None, :, :],
        basis[:, jnp.clip(lag_index - 1, 0, LAG - 1)],
        jnp.zeros((), jnp.bfloat16),
    )
    history_blocks = jnp.einsum(
        "bkw,wu->bku", toeplitz, extended, preferred_element_type=jnp.float32
    )
    mixed = jnp.sum(coupling_mix[:, None, None] * history_blocks, axis=0).astype(jnp.bfloat16)
    mixed_tiles = mixed.reshape(time_dev, tiles_dev, TILE)
    slot_count = unit_count * CAP
    flat_target = coupling_target.reshape(-1)
    entry_count = flat_target.shape[0]
    owner = flat_target // tiles_dev
    local_tile = flat_target % tiles_dev
    entry_index = jnp.arange(entry_count, dtype=jnp.int32)
    same_tile = flat_target[:, None] == flat_target[None, :]
    first_seen = jnp.logical_not(
        jnp.any(same_tile & (entry_index[None, :] < entry_index[:, None]), axis=1)
    )
    lower_rank = (
        (owner[:, None] == owner[None, :])
        & (local_tile[None, :] < local_tile[:, None])
        & first_seen[None, :]
    )
    slot_of = owner * CAP + jnp.sum(lower_rank.astype(jnp.int32), axis=1)
    slot_hit = slot_of[None, :] == jnp.arange(slot_count, dtype=jnp.int32)[:, None]
    slot_ids = jnp.max(jnp.where(slot_hit, local_tile[None, :], -1), axis=1)
    slot_table = slot_hit.reshape(slot_count, tiles_dev, FAN).astype(jnp.bfloat16)
    slot_weight = jnp.einsum(
        "csf,sfkn->cskn", slot_table, coupling_weight, preferred_element_type=jnp.float32
    ).astype(jnp.bfloat16)
    partials = jnp.einsum(
        "tsk,cskn->ctn", mixed_tiles, slot_weight, preferred_element_type=jnp.float32
    ).astype(jnp.bfloat16)
    received, received_ids = (
        lax.all_to_all(
            partials.reshape(unit_count, CAP, time_dev, TILE),
            "unit",
            split_axis=0,
            concat_axis=0,
            tiled=True,
        ),
        lax.all_to_all(
            slot_ids.reshape(unit_count, CAP), "unit", split_axis=0, concat_axis=0, tiled=True
        ),
    )
    flat_ids = received_ids.reshape(-1)
    placing = (flat_ids[None, :] == jnp.arange(tiles_dev, dtype=jnp.int32)[:, None]).astype(
        jnp.bfloat16
    )
    coupling = jnp.einsum(
        "jc,ctn->tjn",
        placing,
        received.reshape(slot_count, time_dev, TILE),
        preferred_element_type=jnp.float32,
    ).reshape(time_dev, units_dev)
    drive = jnp.einsum("tc,uc->tu", stimulus, stim_filter, preferred_element_type=jnp.float32)
    logit = (
        bias[None, :] + drive + jnp.sum(history_blocks * hist_weight[:, None, :], axis=0) + coupling
    )
    resid = spikes.astype(jnp.float32) - jnp.exp(logit)
    resid_bf = resid.astype(jnp.bfloat16)
    bias_total, hist_total = lax.psum(
        (jnp.sum(resid, axis=0), jnp.sum(history_blocks * resid[None, :, :], axis=1)), "tm"
    )
    grad_bias = bias_total / time_total
    grad_hist = hist_total / time_total
    everyone = lax.all_gather(resid_bf, "unit", axis=1, tiled=True)
    picking = (
        flat_target[:, None] == jnp.arange(tiles_dev * unit_count, dtype=jnp.int32)[None, :]
    ).astype(jnp.bfloat16)
    selected = jnp.einsum(
        "ej,tjn->ten",
        picking,
        everyone.reshape(time_dev, tiles_dev * unit_count, TILE),
        preferred_element_type=jnp.float32,
    ).astype(jnp.bfloat16)
    selected = selected.reshape(time_dev, tiles_dev, FAN, TILE)
    coupling_terms = jnp.einsum(
        "tsk,tsfn->sfkn", mixed_tiles, selected, preferred_element_type=jnp.float32
    )
    grad_coupling = (
        lax.psum_scatter(coupling_terms, "tm", scatter_dimension=2, tiled=True) / time_total
    )
    swapped = lax.all_to_all(resid_bf, "tm", split_axis=1, concat_axis=0, tiled=True)
    stim_total = jnp.einsum(
        "tu,tc->uc",
        swapped,
        lax.all_gather(stimulus, "tm", axis=0, tiled=True),
        preferred_element_type=jnp.float32,
    )
    grad_stim = stim_total / time_total
    return (grad_bias, grad_hist, grad_stim, grad_coupling)


def solution(mesh):
    return jax.shard_map(
        shards,
        mesh=mesh,
        in_specs=(
            P("tm", "unit"),
            P("tm", None),
            P("unit"),
            P(None, "unit"),
            P("unit", None),
            P(),
            P("unit", None),
            P("unit", None, None, None),
        ),
        out_specs=(
            P("unit"),
            P(None, "unit"),
            P(("unit", "tm"), None),
            P("unit", None, "tm", None),
        ),
        check_vma=False,
    )
```

profile of v0, /device:TPU:0, one launch (start us, length us, event | category | flops | bytes accessed | tf_op | source)
XLA Modules:
  0.0 1558.2 jit_solution(9174571685299612197)
XLA Ops:
  7.2 1.9 convert_element_type.65
  9.1 1.0 copy-done.6
  10.1 1.3 collective-permute-start
  11.5 0.1 copy.69
  11.5 0.1 reshape.254
  11.6 0.2 fusion.23
  11.8 0.2 convert_reduce_fusion
  12.0 0.1 select_reduce_fusion
  12.1 0.7 all_to_all.24
  12.8 7.6 all-to-all-start.1
  20.5 0.1 reduce_sum.59
  20.5 1.5 compare_select_fusion
  22.0 1.4 reshape.262
  23.4 1.2 broadcast_clamp_fusion
  24.7 0.2 fusion.30
  24.9 5.2 convert_bitcast_fusion
  30.1 0.1 divide_convert_fusion
  30.2 0.1 copy.67
  30.3 1133.5 %gather_fusion = bf16[327680,10]{1,0:T(8,128)(2,1)} fusion(bf16[10,128]{0,1:T(8,128)(2,1)S(1)} %copy.67, s32[327680]{0:T(1024)S(1)} %copy-done.5), kind=kCustom, calls=%fused_computation | custom fusion | bytes 14417920 | tf_op jit(solution)/shard_map/gather | solution.py:52
  1163.8 62.6 %copy.68 = bf16[512,640,10]{1,0,2:T(8,128)(2,1)} copy(bf16[512,640,10]{2,1,0:T(8,128)(2,1)} %bitcast) | data formatting | bytes 13107200 | tf_op jit(solution)/shard_map/gather | solution.py:52
  1226.4 0.4 fusion.20
  1226.8 16.5 %multiply_reduce_fusion.2 = (f32[512,1024]{1,0:T(8,128)S(1)}, bf16[512,1024]{1,0:T(8,128)(2,1)}, f32[10,512,1024]{2,1,0:T(8,128)}) fusion(f32[10,1024]{1,0:T(8,128)S(1)} %copy-done.12, f32[10]{0:T(128)S(1)} %copy-done.13, bf16[512,1024]{1,0:T(8,128)(2,1)S(1)} %copy-done.7, bf16[128,1024]{1,0:T(8,128)(2,1)S(1)} %collective-permute-done, ...), kind=kOutput, calls=%fused_computation.3 | convolution fusion | flops 6736707584 | bytes 32350248 | tf_op jit(solution)/shard_map/bkw,wu->bku/dot_general | solution.py:55
  1243.3 1.5 copy.75
  1244.8 22.9 %bitcast_convert_fusion = bf16[32,128,512]{2,1,0:T(8,128)(2,1)} fusion(bf16[512,8,128,1]{0,2,1,3:T(8,128)(2,1)S(1)} %bitcast.77, bf16[32,8,128,128]{3,0,2,1:T(8,128)(2,1)} %convert_bitcast_fusion), kind=kOutput, calls=%fused_computation.4 | convolution fusion | flops 4297064448 | bytes 13631488 | tf_op jit(solution)/shard_map/tsk,cskn->ctn/dot_general | solution.py:82
  1267.7 7.3 all-to-all-start
  1275.0 0.0 all-gather.2.cloned.1.call-start
  1275.1 0.5 broadcast.315
  1275.6 0.7 reduce.3
  1276.2 0.1 eq.82
  1276.3 54.8 %all-to-all-done = bf16[16,2,512,128]{2,3,1,0:T(8,128)(2,1)} async-done(((bf16[16,2,512,128]{2,3,1,0:T(8,128)(2,1)}), bf16[16,2,512,128]{2,3,1,0:T(8,128)(2,1)}, u32[]{:S(2)}, u32[]{:S(2)}) %all-to-all-start) | async-done | bytes 4194336 | tf_op jit(solution)/shard_map/all_to_all | solution.py:86
  1331.2 11.3 copy.78
  1342.5 3.0 fusion.36
  1345.5 2.6 fusion.41
  1348.2 122.4 %all-gather.2.cloned.1.call-done = bf16[512,16384]{1,0:T(8,128)(2,1)} async-done(((bf16[512,1024]{1,0:T(8,128)(2,1)}), bf16[512,16384]{1,0:T(8,128)(2,1)}) %all-gather.2.cloned.1.call-update) | async-done | bytes 16777232 | tf_op jit(solution)/shard_map/all_gather | solution.py:118
  1470.6 9.8 copy.94
  1480.4 2.6 convolution_convert_fusion
  1483.0 2.1 fusion.13
  1485.0 2.1 copy.83
  1487.1 14.9 all_gather.6
  1502.0 1.2 copy_bitcast_fusion
  1503.2 4.2 all-to-all-start.2
  1507.5 8.7 multiply_reduce_fusion
  1516.2 29.8 %all-reduce = (f32[1024]{0:T(1024)S(1)}, f32[10,1024]{1,0:T(8,128)S(1)}) all-reduce(f32[1024]{0:T(1024)S(1)} %get-tuple-element.29, f32[10,1024]{1,0:T(8,128)S(1)} %multiply_reduce_fusion), channel_id=1, replica_groups=mesh['unit'=16,'tm'=8] {'tm'}, use_global_device_ids=true, to_apply=%region_7.8 | all-reduce | flops 11264 | bytes 90112 | tf_op jit(solution)/shard_map/psum | solution.py:113
  1546.0 0.6 broadcast_multiply_fusion.2
  1546.6 0.6 broadcast_multiply_fusion.1
  1547.2 2.3 convolution_multiply_fusion
  1549.6 1.0 broadcast_multiply_fusion
  1550.5 0.9 copy.84
  (42 shorter events, 0.2 us)
Async XLA Ops:
  7.2 17.7 %copy-start = (bf16[8,4,128,128]{3,2,1,0:T(8,128)(2,1)S(1)}, bf16[8,4,128,128]{3,2,1,0:T(8,128)(2,1)}, u32[]{:S(2)}) copy-start(bf16[8,4,128,128]{3,2,1,0:T(8,128)(2,1)} %param.15) | copy-start | bytes 3145732
  7.2 4.3 copy-start.11
  9.1 1.0 copy-start.6
  10.1 1216.7 %collective-permute-start = (bf16[128,1024]{1,0:T(8,128)(2,1)S(1)}, bf16[128,1024]{1,0:T(8,128)(2,1)S(1)}, u32[]{:S(2)}, u32[]{:S(2)}) collective-permute-start(bf16[128,1024]{1,0:T(8,128)(2,1)S(1)} %slice.6), channel_id=1, source_target_pairs={{0,1},{1,2},{2,3},{3,4},{4,5},{5,6},{6,7},{8,9},{9,10},{10,11},{11... | collective-permute-start | bytes 786440 | tf_op jit(solution)/shard_map/ppermute | solution.py:17
  12.8 1254.9 %all-to-all-start.1 = ((s32[16,1,2]{2,1,0:T(1,128)}), s32[16,1,2]{2,1,0:T(1,128)S(1)}, u32[]{:S(2)}, u32[]{:S(2)}) async-start(s32[16,1,2]{2,1,0:T(1,128)} %bitcast.13), calls=%async_computation.1 | async-start | bytes 16384 | tf_op jit(solution)/shard_map/all_to_all | solution.py:93
  24.9 5.4 copy-start.5
  1163.8 63.0 %copy-start.7 = (bf16[512,1024]{1,0:T(8,128)(2,1)S(1)}, bf16[512,1024]{1,0:T(8,128)(2,1)}, u32[]{:S(2)}) copy-start(bf16[512,1024]{1,0:T(8,128)(2,1)} %copy-done.6) | copy-start | bytes 3145732
  1163.8 63.0 %copy-start.12 = (f32[10,1024]{1,0:T(8,128)S(1)}, f32[10,1024]{1,0:T(8,128)}, u32[]{:S(2)}) copy-start(f32[10,1024]{1,0:T(8,128)} %param.11) | copy-start | bytes 122884
  1163.8 63.0 %copy-start.13 = (f32[10]{0:T(128)S(1)}, f32[10]{0:T(128)}, u32[]{:S(2)}) copy-start(f32[10]{0:T(128)} %param.13) | copy-start | bytes 124
  1267.7 63.4 %all-to-all-start = ((bf16[16,2,512,128]{2,3,1,0:T(8,128)(2,1)}), bf16[16,2,512,128]{2,3,1,0:T(8,128)(2,1)}, u32[]{:S(2)}, u32[]{:S(2)}) async-start(bf16[16,2,512,128]{2,3,1,0:T(8,128)(2,1)} %bitcast.76), calls=%async_computation | async-start | bytes 8388608 | tf_op jit(solution)/shard_map/all_to_all | solution.py:86
  1275.0 195.6 %all-gather.2.cloned.1.call-start = ((), (), s32[]{:S(2)}) async-start(), calls=%async_computation.4 | async-start | bytes 17825792 | tf_op jit(solution)/shard_map/all_gather | solution.py:118
  1342.5 3.0 copy-start.3
  1342.5 3.0 copy-start.8
  1342.5 3.0 copy-start.9
  1342.5 3.0 copy-start.10
  1348.1 201.4 %reduce-scatter.2.cloned.1.call-start = ((), (), s32[]{:S(2)}) async-start(), calls=%async_computation.5 | async-start | bytes 2359296 | tf_op jit(solution)/shard_map/reduce_scatter | solution.py:133
  1487.1 15.0 copy-start.2
  1502.0 5.4 copy-start.4
  1503.2 44.0 %all-to-all-start.2 = ((bf16[512,8,128]{2,0,1:T(8,128)(2,1)}), bf16[512,8,128]{2,0,1:T(8,128)(2,1)}, u32[]{:S(2)}, u32[]{:S(2)}) async-start(bf16[512,8,128]{2,0,1:T(8,128)(2,1)} %copy_bitcast_fusion), calls=%async_computation.2 | async-start | bytes 2097152 | tf_op jit(solution)/shard_map/all_to_all | solution.py:135
  1507.5 43.9 %copy-start.1 = (bf16[8,4,128,128]{3,2,1,0:T(8,128)(2,1)S(1)}, bf16[8,4,128,128]{3,2,1,0:T(8,128)(2,1)}, u32[]{:S(2)}) copy-start(bf16[8,4,128,128]{3,2,1,0:T(8,128)(2,1)} %param.15) | copy-start | bytes 3145732
Sparse Core Ops, SparseCore 0:
  1348.3 122.2 all-gather.1
  1487.2 41.0 reduce-scatter.1
where the time goes:
time: 1560 us
  local copies, waits for them, and re-layouts  1230 us (79%)
  waiting for transfers between devices  177 us (11%)
  matrix products  57.1 us (4%)
  blocking collectives  44.7 us (3%)
  starting transfers between devices  20.5 us (1%)
  other arithmetic  17.5 us (1%)
    gather x2, local copies, waits for them, and re-layouts, shards(): basis[:, jnp.clip(lag_index - 1, 0, LAG - 1)]  1200 us
    all_gather x1, waiting for transfers between devices, shards(): everyone = lax.all_gather(resid_bf, 'unit', axis=1, tiled=True)  122 us
    all_to_all x1, waiting for transfers between devices, shards(): lax.all_to_all(partials.reshape(unit_count, CAP, time_dev, TILE), 'unit',...  54.8 us
  transfers between devices with their start and end apart: 6, of which 2 were waited for; matrix products, arithmetic and copies ran while one was open for 81% of the time, Pallas kernels for 0%

commit v1 on v0

--- a/solution.py
+++ b/solution.py
@@ -115,7 +115,9 @@
     )
     grad_bias = bias_total / time_total
     grad_hist = hist_total / time_total
-    everyone = lax.all_gather(resid_bf, "unit", axis=1, tiled=True)
+    everyone = jnp.concatenate(
+        lax.all_to_all(jnp.stack([resid_bf] * lax.axis_size("unit")), "unit", 0, 0), axis=1
+    )
     picking = (
         flat_target[:, None] == jnp.arange(tiles_dev * unit_count, dtype=jnp.int32)[None, :]
     ).astype(jnp.bfloat16)

time: 1560 us -> 1690 us (1.083)
  blocking collectives: 44.7 us -> 248 us
  waiting for transfers between devices: 177 us -> 55 us
  local copies, waits for them, and re-layouts: 1230 us -> 1270 us
    all_to_all x0 -> x1, blocking collectives: none -> 201 us  [shards(): lax.all_to_all(jnp.stack([resid_bf] * lax.axis_size('unit')), 'unit', 0, 0)]
    all_gather x1 -> x0, waiting for transfers between devices: 122 us -> none  [shards(): everyone = lax.all_gather(resid_bf, 'unit', axis=1, tiled=True)]
    another operation x0 -> x2, local copies, waits for them, and re-layouts: none -> 27.5 us  [the longest x1 25.3 us: shards(): everyone.reshape(time_dev, tiles_dev * unit_count, TILE)]
    reshape x0 -> x1, local copies, waits for them, and re-layouts: none -> 26.9 us  [shards(): jnp.concatenate(lax.all_to_all(jnp.stack([resid_bf] * lax.axis_size('unit...]
  transfers between devices with their start and end apart: 6 -> 5, of which waited for: 2 -> 1; matrix products, arithmetic and copies ran while one was open for 81% -> 75% of each run, Pallas kernels for 0% -> 0%
where the time goes in v1:
time: 1690 us
  local copies, waits for them, and re-layouts  1270 us (75%)
  blocking collectives  248 us (15%)
  matrix products  64.7 us (4%)
  waiting for transfers between devices  55 us (3%)
  starting transfers between devices  21.1 us (1%)
  other arithmetic  17.5 us (1%)
    gather x2, local copies, waits for them, and re-layouts, shards(): basis[:, jnp.clip(lag_index - 1, 0, LAG - 1)]  1200 us
    all_to_all x1, blocking collectives, shards(): lax.all_to_all(jnp.stack([resid_bf] * lax.axis_size('unit')), 'unit', 0, 0)  201 us
    all_to_all x1, waiting for transfers between devices, shards(): lax.all_to_all(partials.reshape(unit_count, CAP, time_dev, TILE), 'unit',...  55 us
  transfers between devices with their start and end apart: 5, of which 1 were waited for; matrix products, arithmetic and copies ran while one was open for 75% of the time, Pallas kernels for 0%

profile of v1, /device:TPU:0, one launch (start us, length us, event | category | flops | bytes accessed | tf_op | source)
XLA Modules:
  0.0 1691.9 jit_solution(5420108988795752303)
XLA Ops:
  7.2 1.9 convert_element_type.65
  9.1 0.7 slice.6
  9.8 2.0 collective-permute-start
  11.9 0.1 reshape.256
  12.0 0.2 fusion.23
  12.2 0.2 convert_reduce_fusion
  12.4 0.1 select_reduce_fusion
  12.5 0.7 all_to_all.27
  13.2 7.6 all-to-all-start.1
  20.9 1.5 compare_select_fusion
  22.4 1.4 reshape.264
  23.8 1.2 broadcast_clamp_fusion
  25.1 0.2 fusion.30
  25.3 5.2 convert_bitcast_fusion
  30.5 0.1 divide_convert_fusion
  30.6 0.1 copy.69
  30.7 1133.5 %gather_fusion = bf16[327680,10]{1,0:T(8,128)(2,1)} fusion(bf16[10,128]{0,1:T(8,128)(2,1)S(1)} %copy.69, s32[327680]{0:T(1024)S(1)} %copy-done.3), kind=kCustom, calls=%fused_computation | custom fusion | bytes 14417920 | tf_op jit(solution)/shard_map/gather | solution.py:52
  1164.2 62.6 %copy.70 = bf16[512,640,10]{1,0,2:T(8,128)(2,1)} copy(bf16[512,640,10]{2,1,0:T(8,128)(2,1)} %bitcast) | data formatting | bytes 13107200 | tf_op jit(solution)/shard_map/gather | solution.py:52
  1226.8 0.4 fusion.20
  1227.2 18.6 %multiply_reduce_fusion.2 = (f32[512,1024]{1,0:T(8,128)}, bf16[512,1024]{1,0:T(8,128)(2,1)S(1)}, f32[10,512,1024]{2,1,0:T(8,128)}) fusion(f32[10,1024]{1,0:T(8,128)S(1)} %copy-done.11, f32[10]{0:T(128)S(1)} %copy-done.12, bf16[512,1024]{1,0:T(8,128)(2,1)S(1)} %convert_element_type.65, bf16[128,1024]{1,0:T(8,128)(2,1)} %collective-permute-done, ...), kind=kOutput, calls=%fused_computation.3 | convolution fusion | flops 6736707584 | bytes 32350248 | tf_op jit(solution)/shard_map/bkw,wu->bku/dot_general | solution.py:55
  1245.7 0.5 copy.77
  1246.3 23.1 %bitcast_convert_fusion = bf16[32,128,512]{2,1,0:T(8,128)(2,1)} fusion(bf16[512,8,128,1]{0,2,1,3:T(8,128)(2,1)S(1)} %bitcast.75, bf16[32,8,128,128]{3,0,2,1:T(8,128)(2,1)} %convert_bitcast_fusion), kind=kOutput, calls=%fused_computation.4 | convolution fusion | flops 4297064448 | bytes 13631488 | tf_op jit(solution)/shard_map/tsk,cskn->ctn/dot_general | solution.py:82
  1269.4 7.3 all-to-all-start
  1276.7 0.5 broadcast.317
  1277.2 0.7 reduce.3
  1277.9 0.1 eq.82
  1277.9 55.0 %all-to-all-done = bf16[16,2,512,128]{2,3,1,0:T(8,128)(2,1)} async-done(((bf16[16,2,512,128]{2,3,1,0:T(8,128)(2,1)}), bf16[16,2,512,128]{2,3,1,0:T(8,128)(2,1)}, u32[]{:S(2)}, u32[]{:S(2)}) %all-to-all-start) | async-done | bytes 4194336 | tf_op jit(solution)/shard_map/all_to_all | solution.py:86
  1333.0 11.3 copy.80
  1344.3 3.0 fusion.36
  1347.3 0.5 copy-done.4
  1347.7 1.0 fusion.41
  1348.7 2.2 stack.2
  1350.9 201.1 %all_to_all.38 = bf16[16,512,1024]{2,1,0:T(8,128)(2,1)S(1)} all-to-all(bf16[16,512,1024]{2,1,0:T(8,128)(2,1)S(1)} %stack.2), channel_id=1, replica_groups=mesh['unit'=16,'tm'=8] {'unit'}, dimensions={0} | all-to-all | bytes 33554432 | tf_op jit(solution)/shard_map/all_to_all | solution.py:119
  1552.0 26.9 %copy.83 = bf16[512,16,1024]{2,1,0:T(8,128)(2,1)} copy(bf16[512,16,1024]{2,0,1:T(8,128)(2,1)S(1)} %bitcast.70) | data formatting | bytes 33554432 | tf_op jit(solution)/shard_map/reshape | solution.py:118
  1578.9 25.3 %reshape_reshape.3 = bf16[512,128,128]{2,1,0:T(8,128)(2,1)} reshape(bf16[512,16,1024]{2,1,0:T(8,128)(2,1)} %copy.83) | data formatting | bytes 33554432 | tf_op jit(solution)/shard_map/reshape;reshape | solution.py:127
  1604.2 8.2 convolution_convert_fusion
  1612.4 3.4 fusion.13
  1615.8 3.1 copy.86
  1619.0 17.1 %all_gather.3 = bf16[4096,64]{0,1:T(8,128)(2,1)} all-gather(bf16[512,64]{0,1:T(8,128)(2,1)S(1)} %copy-done.7), channel_id=1, replica_groups=mesh['unit'=16,'tm'=8] {'tm'}, dimensions={0}, use_global_device_ids=true | all-gather | bytes 589824 | tf_op jit(solution)/shard_map/all_gather | solution.py:141
  1636.1 1.2 copy_bitcast_fusion
  1637.2 4.2 all-to-all-start.2
  1641.5 8.7 multiply_reduce_fusion
  1650.2 29.5 %all-reduce = (f32[1024]{0:T(1024)S(1)}, f32[10,1024]{1,0:T(8,128)S(1)}) all-reduce(f32[1024]{0:T(1024)S(1)} %get-tuple-element.29, f32[10,1024]{1,0:T(8,128)S(1)} %multiply_reduce_fusion), channel_id=1, replica_groups=mesh['unit'=16,'tm'=8] {'tm'}, use_global_device_ids=true, to_apply=%region_7.8 | all-reduce | flops 11264 | bytes 90112 | tf_op jit(solution)/shard_map/psum | solution.py:113
  1679.7 0.6 broadcast_multiply_fusion.2
  1680.3 0.6 broadcast_multiply_fusion.1
  1680.9 2.3 convolution_multiply_fusion
  1683.3 1.0 broadcast_multiply_fusion
  1684.2 0.9 copy.87
  (40 shorter events, 0.3 us)
Async XLA Ops:
  7.2 18.1 %copy-start = (bf16[8,4,128,128]{3,2,1,0:T(8,128)(2,1)S(1)}, bf16[8,4,128,128]{3,2,1,0:T(8,128)(2,1)}, u32[]{:S(2)}) copy-start(bf16[8,4,128,128]{3,2,1,0:T(8,128)(2,1)} %param.15) | copy-start | bytes 3145732
  7.2 4.7 copy-start.10
  9.8 1217.3 %collective-permute-start = (bf16[128,1024]{1,0:T(8,128)(2,1)}, bf16[128,1024]{1,0:T(8,128)(2,1)}, u32[]{:S(2)}, u32[]{:S(2)}) collective-permute-start(bf16[128,1024]{1,0:T(8,128)(2,1)} %slice.6), channel_id=1, source_target_pairs={{0,1},{1,2},{2,3},{3,4},{4,5},{5,6},{6,7},{8,9},{9,10},{10,11},{11... | collective-permute-start | bytes 786440 | tf_op jit(solution)/shard_map/ppermute | solution.py:17
  13.2 1256.1 %all-to-all-start.1 = ((s32[16,1,2]{2,1,0:T(1,128)}), s32[16,1,2]{2,1,0:T(1,128)S(1)}, u32[]{:S(2)}, u32[]{:S(2)}) async-start(s32[16,1,2]{2,1,0:T(1,128)} %bitcast.13), calls=%async_computation.1 | async-start | bytes 16384 | tf_op jit(solution)/shard_map/all_to_all | solution.py:93
  25.3 5.4 copy-start.3
  1164.2 62.9 %copy-start.11 = (f32[10,1024]{1,0:T(8,128)S(1)}, f32[10,1024]{1,0:T(8,128)}, u32[]{:S(2)}) copy-start(f32[10,1024]{1,0:T(8,128)} %param.11) | copy-start | bytes 122884
  1164.2 63.0 %copy-start.12 = (f32[10]{0:T(128)S(1)}, f32[10]{0:T(128)}, u32[]{:S(2)}) copy-start(f32[10]{0:T(128)} %param.13) | copy-start | bytes 124
  1246.3 23.1 %copy-start.5 = (bf16[512,1024]{0,1:T(8,128)(2,1)}, bf16[512,1024]{0,1:T(8,128)(2,1)S(1)}, u32[]{:S(2)}) copy-start(bf16[512,1024]{0,1:T(8,128)(2,1)S(1)} %copy.77) | copy-start | bytes 3145732
  1269.4 63.6 %all-to-all-start = ((bf16[16,2,512,128]{2,3,1,0:T(8,128)(2,1)}), bf16[16,2,512,128]{2,3,1,0:T(8,128)(2,1)}, u32[]{:S(2)}, u32[]{:S(2)}) async-start(bf16[16,2,512,128]{2,3,1,0:T(8,128)(2,1)} %bitcast.74), calls=%async_computation | async-start | bytes 8388608 | tf_op jit(solution)/shard_map/all_to_all | solution.py:86
  1276.6 406.6 %reduce-scatter.2.cloned.1.call-start = ((), (), s32[]{:S(2)}) async-start(), calls=%async_computation.5 | async-start | bytes 2359296 | tf_op jit(solution)/shard_map/reduce_scatter | solution.py:135
  1344.2 3.0 copy-start.2
  1344.2 3.5 copy-start.4
  1344.2 3.5 copy-start.7
  1344.2 3.5 copy-start.8
  1344.3 3.5 copy-start.9
  1604.2 8.2 copy-start.6
  1637.2 43.7 %all-to-all-start.2 = ((bf16[512,8,128]{2,0,1:T(8,128)(2,1)}), bf16[512,8,128]{2,0,1:T(8,128)(2,1)}, u32[]{:S(2)}, u32[]{:S(2)}) async-start(bf16[512,8,128]{2,0,1:T(8,128)(2,1)} %copy_bitcast_fusion), calls=%async_computation.2 | async-start | bytes 2097152 | tf_op jit(solution)/shard_map/all_to_all | solution.py:137
  1641.5 43.6 %copy-start.1 = (bf16[8,4,128,128]{3,2,1,0:T(8,128)(2,1)S(1)}, bf16[8,4,128,128]{3,2,1,0:T(8,128)(2,1)}, u32[]{:S(2)}) copy-start(bf16[8,4,128,128]{3,2,1,0:T(8,128)(2,1)} %param.15) | copy-start | bytes 3145732
Sparse Core Ops, SparseCore 0:
  1619.1 42.4 reduce-scatter.1
